TPU v7x, 256 devices: a whole 4x4x8 slice. The times are simulated.
256 devices in a mesh: section: 4 (over x_hi, core), fsdp: 64 (over z, x_lo, y).
Axes of the slice: x: 4 (x_hi: 2, x_lo: 2; x = x_hi * 2 + x_lo), y: 4, z: 8, core: 2. Of those that a mesh axis runs over, the one named last changes fastest.
Arguments:
- signals: bfloat16 [16384, 1536], P('fsdp', 'section'), may hold values from -6 to 6
- conv_weight: bfloat16 [768, 9, 1536], P('fsdp', None, 'section'), may hold values from -0.078125 to 0.078125
- buckets: int32 [2, 2], replicated, may hold values from 0 to 8, as said below
Outputs:
- results: bfloat16 [16384, 1536], P('fsdp', 'section')
- grad_weight: float32 [768, 9, 1536], P('fsdp', None, 'section')
Inputs may be any that keep to these rules, and one draw needn't show every extreme that they name: `buckets`: a bucket b means 16 + 2 b live pixels along that side, in the top left of each sample's grid; microbatch 0 has a height bucket of 5 or more; some entry is 8.
All inputs are finite; a program needn't handle non-finite values.
Results may differ from a plain program's by a relative error of at most 0.0054.
Values may be sent and summed in bfloat16 or wider, within the bound.
No kernel may reach another device: no remote copies, remote signals or barrier semaphores. Data moves between devices by JAX's collectives and lax.ppermute only.
A program may use at most 128 MiB of HBM per device.

v0:
```python
import jax
import jax.numpy as jnp
from jax import lax
from jax.sharding import Mesh
from jax.sharding import PartitionSpec as P

GROUPS = 32
SIDE = 32
MICRO = 2
ROWS_DEV = 8
FSDP = ("fsdp_0", "fsdp_1", "fsdp_2")
eps = 1e-05


def from_partner(value, axis, stride):
    mask = 2**stride
    pairs = [(source, source ^ mask) for source in range(lax.axis_size(axis))]
    return lax.ppermute(value, axis, pairs)


def padded_2(cells, sides, width):
    for axis, dim in sides:
        count = lax.axis_size(axis)
        head = lax.slice_in_dim(cells, 0, width, axis=dim)
        tail = lax.slice_in_dim(cells, cells.shape[dim] - width, cells.shape[dim], axis=dim)
        cells = jnp.concatenate(
            [
                lax.ppermute(tail, axis, [(i, (i + 1) % count) for i in range(count)]),
                cells,
                lax.ppermute(head, axis, [((i + 1) % count, i) for i in range(count)]),
            ],
            axis=dim,
        )
    return cells


def copy_for_each(shard, axis):
    copies = jnp.broadcast_to(shard, (lax.axis_size(axis), *shard.shape))
    return lax.all_to_all(copies, axis, split_axis=0, concat_axis=0, tiled=True)


def over_copies(shard, axis):
    everything = copy_for_each(shard, axis)
    return jnp.sum(everything, axis=0)


def together(arrays, axis):
    ends = [0]
    for a in arrays:
        ends.append(ends[-1] + a.size)
    subtotal = over_copies(jnp.concatenate([a.ravel() for a in arrays]), axis)
    return tuple((subtotal[b:e].reshape(a.shape) for a, b, e in zip(arrays, ends, ends[1:])))


def reduced_to_own(tiles, axes, turns):
    dims = [lax.axis_size(a) for a in axes]
    tiles = tiles.reshape(*dims, *tiles.shape[1:])
    tiles = tiles.transpose(*turns, *range(len(axes), tiles.ndim))
    tiles = tiles.reshape(-1, *tiles.shape[len(axes) :])
    for k in turns:
        tiles = lax.psum_scatter(tiles, axes[k], scatter_dimension=0, tiled=True)
    return tiles[0]


def split_up(shard, dim, length):
    dims = shard.shape
    tiles = shard.reshape(*dims[:dim], length, dims[dim] // length, *dims[dim + 1 :])
    return jnp.moveaxis(tiles, dim, 0)


def sum_by_axis(shard, axes, turns, dim):
    length = lax.axis_size(axes)
    return reduced_to_own(split_up(shard, dim, length), axes, turns)


def silu_slope(value):
    sig = jax.nn.sigmoid(value)
    return sig * (1.0 + value * (1.0 - sig))


def section_swap(value, bit):
    return from_partner(value, "section", bit)


def per_device(signals, conv_weight, buckets):
    tok = signals.shape[0]
    half = signals.shape[1]
    width = 2 * half
    group_width = width // GROUPS
    local_groups = half // group_width
    section_index = lax.axis_index("section")
    upper_half = section_index % 2 == 1
    role_up = section_index >= 2
    fsdp_index = lax.axis_index(FSDP)
    pieces = SIDE // ROWS_DEV
    samples = lax.axis_size(FSDP) // pieces
    shifted = fsdp_index + 1
    sample_id = shifted // pieces % samples
    piece_id = shifted % pieces
    micro_id = sample_id // (samples // MICRO)
    picked_micro = jnp.arange(MICRO) == micro_id
    bucket_h = jnp.sum(jnp.where(picked_micro, buckets[:, 0], 0))
    bucket_w = jnp.sum(jnp.where(picked_micro, buckets[:, 1], 0))
    live_h = 16 + 2 * bucket_h
    live_w = 16 + 2 * bucket_w
    row_ids = piece_id * ROWS_DEV + jnp.arange(ROWS_DEV)
    col_ids = jnp.arange(SIDE)
    mask_grid = ((row_ids[:, None] < live_h) & (col_ids[None, :] < live_w)).astype(jnp.float32)
    mask_flat = mask_grid.reshape(tok, 1)
    group_count = (live_h * live_w).astype(jnp.float32) * group_width
    sample_hot = (jnp.arange(samples) == sample_id).astype(jnp.float32)[:, None]

    def with_rims(field):
        grid = field.reshape(ROWS_DEV, SIDE, field.shape[-1])
        padded = padded_2(grid, ((FSDP, 0),), 1)
        top = jnp.where(piece_id > 0, padded[:1], jnp.zeros_like(padded[:1]))
        bottom = jnp.where(piece_id < pieces - 1, padded[-1:], jnp.zeros_like(padded[-1:]))
        padded = jnp.concatenate([top, padded[1:-1], bottom], axis=0)
        return jnp.pad(padded, ((0, 0), (1, 1), (0, 0)))

    def group_totals(first, second):
        total_first, total_second = together(
            (sample_hot * first[None, :], sample_hot * second[None, :]), FSDP
        )
        return (
            jnp.sum(sample_hot * total_first, axis=0),
            jnp.sum(sample_hot * total_second, axis=0),
        )

    def normalize(values):
        grouped = values.reshape(tok, local_groups, group_width)
        masked = grouped * mask_flat[:, :, None]
        first = jnp.sum(masked, axis=(0, 2))
        second = jnp.sum(masked * masked, axis=(0, 2))
        total_first, total_second = group_totals(first, second)
        mean = total_first / group_count
        spread = total_second / group_count - mean * mean
        scale = lax.rsqrt(spread + eps)
        normed = (grouped - mean[None, :, None]) * scale[None, :, None]
        return (normed.reshape(tok, half), scale)

    def forward(inputs, weights):
        values = inputs.astype(jnp.float32)
        normed, scale = normalize(values)
        activated = (mask_flat * jax.nn.silu(normed)).astype(jnp.bfloat16)
        padded = with_rims(activated)
        partner = section_swap(padded, 0)
        lower = jnp.where(upper_half, partner, padded)
        upper = jnp.where(upper_half, padded, partner)
        full = jnp.concatenate([lower, upper], axis=-1)
        mixed = jnp.zeros((tok, half), jnp.float32)
        for tap in range(9):
            row_off, col_off = (tap // 3, tap % 3)
            slab = full[row_off : row_off + ROWS_DEV, col_off : col_off + SIDE].reshape(tok, width)
            mixed = mixed + jnp.dot(slab, weights[:, tap, :], preferred_element_type=jnp.float32)
        output = (values + mask_flat * mixed).astype(jnp.bfloat16)
        return (output, (normed, scale, full))

    def backward(grads, cache, weights):
        normed, scale, full = cache
        slope = (grads.astype(jnp.float32) * mask_flat).astype(jnp.bfloat16)
        padded = with_rims(slope)
        partial_value = jnp.zeros((tok, width), jnp.float32)
        for tap in range(9):
            row_off, col_off = (tap // 3, tap % 3)
            slab = padded[
                2 - row_off : 2 - row_off + ROWS_DEV, 2 - col_off : 2 - col_off + SIDE
            ].reshape(tok, half)
            partial_value = partial_value + lax.dot_general(
                slab,
                weights[:, tap, :],
                (((1,), (1,)), ((), ())),
                preferred_element_type=jnp.float32,
            )
        keep = jnp.where(upper_half, partial_value[:, half:], partial_value[:, :half])
        send = jnp.where(upper_half, partial_value[:, :half], partial_value[:, half:]).astype(
            jnp.bfloat16
        )
        arrived = section_swap(send, 0)
        kept = lax.optimization_barrier(keep.astype(jnp.bfloat16)).astype(jnp.float32)
        upstream = kept + arrived.astype(jnp.float32)
        gated = mask_flat * upstream * silu_slope(normed)
        grouped = gated.reshape(tok, local_groups, group_width)
        normed_grouped = normed.reshape(tok, local_groups, group_width)
        first = jnp.sum(grouped, axis=(0, 2))
        second = jnp.sum(grouped * normed_grouped, axis=(0, 2))
        total_first, total_second = group_totals(first, second)
        centred = (
            grouped
            - (total_first / group_count)[None, :, None]
            - normed_grouped * (total_second / group_count)[None, :, None]
        )
        through = mask_flat * (scale[None, :, None] * centred).reshape(tok, half)
        return (grads.astype(jnp.float32) + through, slope)

    weights = lax.all_gather(conv_weight, FSDP, axis=0, tiled=True)
    start = (signals.astype(jnp.float32) * mask_flat).astype(jnp.bfloat16)
    first_out, first_cache = forward(start, weights)
    handed = section_swap(first_out, 1)
    second_out, second_cache = forward(handed, weights)
    up_grads, up_slope = backward(signals, second_cache, weights)
    returned = section_swap(up_grads.astype(jnp.bfloat16), 1)
    down_grads, down_slope = backward(returned, first_cache, weights)
    results = jnp.where(role_up, second_out, (mask_flat * down_grads).astype(jnp.bfloat16))
    chosen_full = jnp.where(role_up, second_cache[2], first_cache[2])
    chosen_slope = jnp.where(role_up, up_slope, down_slope)
    taps = []
    for tap in range(9):
        row_off, col_off = (tap // 3, tap % 3)
        slab = chosen_full[row_off : row_off + ROWS_DEV, col_off : col_off + SIDE].reshape(
            tok, width
        )
        taps.append(
            lax.dot_general(
                slab, chosen_slope, (((0,), (0,)), ((), ())), preferred_element_type=jnp.float32
            )
        )
    grad_weight = sum_by_axis(jnp.stack(taps, axis=1), FSDP, (0, 2, 1), 0)
    return (results, grad_weight)


def solution(mesh):
    finer = Mesh(
        mesh.devices.reshape(mesh.shape["section"], 8, 2, 4),
        ("section", "fsdp_0", "fsdp_1", "fsdp_2"),
    )
    placed = (P(FSDP, "section"), P(FSDP, None, "section"), P())
    return jax.shard_map(
        per_device,
        mesh=finer,
        in_specs=placed,
        out_specs=(P(FSDP, "section"), P(FSDP, None, "section")),
        check_vma=False,
    )
```

profile of v0, /device:TPU:1, one launch (start us, length us, event | category | flops | bytes accessed | tf_op | source)
XLA Modules:
  0.0 720.2 jit_solution(4324919274513506607)
XLA Ops:
  7.2 1.6 copy.91
  12.0 1.1 fusion.11
  13.1 9.8 %collective-permute-start.8 = (bf16[1,32,384]{2,1,0:T(8,128)(2,1)S(1)}, bf16[1,32,384]{2,1,0:T(8,128)(2,1)S(1)}, u32[]{:S(2)}, u32[]{:S(2)}) collective-permute-start(bf16[1,32,384]{2,1,0:T(8,128)(2,1)S(1)} %get-tuple-element.96), channel_id=1, source_target_pairs={{1,0},{2,1},{3,2},{4,3},{5,4},{6,5},{7,6},{8,7},{9,8},{10,9},{11,1... | collective-permute-start | bytes 73736 | tf_op jit(solution)/shard_map/ppermute | solution.py:30
  24.3 4.6 all-to-all-start
  30.0 8.2 %collective-permute-done.7 = bf16[1,32,384]{2,1,0:T(8,128)(2,1)S(1)} collective-permute-done((bf16[1,32,384]{2,1,0:T(8,128)(2,1)S(1)}, bf16[1,32,384]{2,1,0:T(8,128)(2,1)S(1)}, u32[]{:S(2)}, u32[]{:S(2)}) %collective-permute-start.7) | collective-permute-done | bytes 24608 | tf_op jit(solution)/shard_map/ppermute | solution.py:28
  40.1 1.7 collective-permute-start.1
  43.2 6.4 collective-permute-done
  49.8 3.6 collective-permute-start.2
  54.8 1.9 fusion.74
  56.7 227.4 %all-gather.2.cloned.1.call-done = bf16[768,9,384]{2,1,0:T(8,128)(2,1)} async-done(((bf16[12,9,384]{2,1,0:T(8,128)(2,1)}), bf16[768,9,384]{2,1,0:T(8,128)(2,1)}) %all-gather.2.cloned.1.call-update) | async-done | bytes 5308432 | tf_op jit(solution)/shard_map/all_gather | solution.py:196
  284.1 20.1 %fusion.92 = (bf16[768,1,384]{2,1,0:T(2,128)(2,1)S(1)}, bf16[768,1,384]{2,1,0:T(2,128)(2,1)S(1)}, bf16[768,1,384]{2,1,0:T(2,128)(2,1)S(1)}, bf16[768,1,384]{2,1,...) fusion(bf16[768,9,384]{2,1,0:T(8,128)(2,1)} %all-gather.2.clone, ...), kind=kLoop, calls=%fused_computation.263 | loop fusion | bytes 10616832 | tf_op jit(solution)/shard_map/slice | solution.py:155
  311.0 3.0 collective-permute-start.3
  318.5 1.3 convolution_add_fusion.8
  323.4 1.3 broadcast_multiply_fusion.5
  324.7 1.4 mul.439
  328.2 7.3 %all-to-all-start.1 = ((f32[64,1,512]{2,1,0:T(1,128)}), f32[64,1,512]{2,1,0:T(1,128)}, u32[]{:S(2)}, u32[]{:S(2)}) async-start(f32[64,1,512]{2,1,0:T(1,128)} %broadcast_in_dim.15), calls=%async_computation.1 | async-start | bytes 262144 | tf_op jit(solution)/shard_map/all_to_all | solution.py:39
  335.5 1.7 convolution_add_fusion.7
  338.0 43.5 %collective-permute-start.9 = (bf16[256,384]{1,0:T(8,128)(2,1)}, bf16[256,384]{1,0:T(8,128)(2,1)}, u32[]{:S(2)}, u32[]{:S(2)}) collective-permute-start(bf16[256,384]{1,0:T(8,128)(2,1)} %get-tuple-element.74), channel_id=1, source_target_pairs={{0,64},{64,0},{128,192},{192,128},{1,65},{65,1},{129,193},{193,129... | collective-permute-start | bytes 589832 | tf_op jit(solution)/shard_map/ppermute | solution.py:18
  383.8 1.3 reshape.497
  388.7 2.5 fusion.87
  393.4 20.4 %all_to_all.24 = f32[64,1,512]{2,1,0:T(1,128)S(1)} all-to-all(f32[64,1,512]{2,1,0:T(1,128)S(1)} %broadcast_in_dim.16), channel_id=1, replica_groups=mesh['section'=4,'fsdp_0'=8,'fsdp_1'=2,'fsdp_2'=4] {'fsdp_0','fsdp_1','f..., dimensions={0} | all-to-all | bytes 262144 | tf_op jit(solution)/shard_map/all_to_all | solution.py:39
  415.7 1.3 fusion.17
  417.0 1.8 collective-permute-start.5
  418.8 1.8 collective-permute-start.10
  420.6 5.2 collective-permute-done.4
  426.7 4.1 collective-permute-start.6
  430.8 1.1 broadcast_select_fusion.4
  432.4 1.2 broadcast_select_fusion
  434.4 1.2 fusion.8
  435.6 1.9 fusion.93
  437.5 1.9 copy.104
  439.5 1.9 dot_general.226
  441.4 1.9 copy.105
  443.3 1.9 dot_general.230
  445.2 1.9 copy.106
  447.1 1.9 dot_general.234
  449.0 1.9 copy.107
  450.9 1.9 dot_general.238
  452.8 1.9 copy.108
  454.7 1.9 dot_general.242
  456.6 1.9 copy.109
  458.5 1.9 dot_general.246
  460.4 1.9 copy.110
  462.3 1.9 dot_general.250
  464.2 1.9 copy.111
  466.1 1.9 dot_general.254
  468.0 1.9 copy.112
  469.9 1.9 dot_general.258
  471.8 1.5 bitcast_dynamic-update-slice_fusion.8
  481.0 11.2 %copy.113 = f32[8,4,2,12,9,384]{5,2,1,0,4,3:T(2,128)} copy(f32[8,4,2,12,9,384]{5,3,1,2,0,4:T(8,128)S(1)} %bitcast.228) | data formatting | bytes 21233664 | tf_op jit(solution)/shard_map/transpose | solution.py:58
  492.3 13.5 %reshape.540 = f32[64,12,9,384]{3,0,2,1:T(8,128)} reshape(f32[8,4,2,12,9,384]{5,2,1,0,4,3:T(2,128)} %copy.113) | data formatting | bytes 21233664 | tf_op jit(solution)/shard_map/reshape | solution.py:59
  508.3 1.2 collective-permute-start.11
  509.6 5.9 collective-permute-done.11
  521.8 4.8 collective-permute-start.13
  526.7 1.5 fusion.65
  530.8 85.7 %reduce-scatter.4.cloned.1.call-done = f32[8,12,9,384]{3,0,2,1:T(8,128)} async-done(((f32[64,12,9,384]{3,0,2,1:T(8,128)}), f32[8,12,9,384]{3,0,2,1:T(8,128)}) %reduce-scatter.4.cloned.1.call-update) | async-done | bytes 1327120 | tf_op jit(solution)/shard_map/reduce_scatter | solution.py:61
  616.6 1.2 fusion.86
  619.2 8.6 %all-to-all-start.3 = ((f32[64,1,512]{2,1,0:T(1,128)}), f32[64,1,512]{2,1,0:T(1,128)S(1)}, u32[]{:S(2)}, u32[]{:S(2)}) async-start(f32[64,1,512]{2,1,0:T(1,128)} %broadcast_in_dim.17), calls=%async_computation.3 | async-start | bytes 262144 | tf_op jit(solution)/shard_map/all_to_all | solution.py:39
  628.2 9.3 %all-to-all-done.3 = f32[64,1,512]{2,1,0:T(1,128)S(1)} async-done(((f32[64,1,512]{2,1,0:T(1,128)}), f32[64,1,512]{2,1,0:T(1,128)S(1)}, u32[]{:S(2)}, u32[]{:S(2)}) %all-to-all-start.3) | async-done | bytes 131104 | tf_op jit(solution)/shard_map/all_to_all | solution.py:39
  637.9 32.5 %all-reduce.9.cloned.1.call-done = f32[8,12,9,384]{3,0,2,1:T(8,128)} async-done(((f32[8,12,9,384]{3,0,2,1:T(8,128)}), f32[8,12,9,384]{3,0,2,1:T(8,128)}) %all-reduce.9.cloned.1.call-update) | async-done | bytes 1327120
  670.5 2.2 constant_dynamic-slice_fusion.1
  673.0 2.2 fusion.7
  675.2 35.8 %all-reduce.11.cloned.1.call-done = f32[2,12,9,384]{3,0,2,1:T(2,128)} async-done(((f32[2,12,9,384]{3,0,2,1:T(2,128)}), f32[2,12,9,384]{3,0,2,1:T(2,128)}) %all-reduce.11.cloned.1.call-update) | async-done | bytes 331792
  711.0 1.7 constant_dynamic-slice_fusion
  (286 shorter events, 60.2 us)
Async XLA Ops:
  7.2 277.0 %all-gather.2.cloned.1.call-start = ((), (), s32[]{:S(2)}) async-start(), calls=%async_computation.5 | async-start | bytes 9584640 | tf_op jit(solution)/shard_map/all_gather | solution.py:196
  13.1 16.9 %collective-permute-start.8 = (bf16[1,32,384]{2,1,0:T(8,128)(2,1)S(1)}, bf16[1,32,384]{2,1,0:T(8,128)(2,1)S(1)}, u32[]{:S(2)}, u32[]{:S(2)}) collective-permute-start(bf16[1,32,384]{2,1,0:T(8,128)(2,1)S(1)} %get-tuple-element.96), channel_id=1, source_target_pairs={{1,0},{2,1},{3,2},{4,3},{5,4},{6,5},{7,6},{8,7},{9,8},{10,9},{11,1... | collective-permute-start | bytes 73736 | tf_op jit(solution)/shard_map/ppermute | solution.py:30
  24.3 14.5 %all-to-all-start = ((f32[64,1,512]{2,1,0:T(1,128)}), f32[64,1,512]{2,1,0:T(1,128)S(1)}, u32[]{:S(2)}, u32[]{:S(2)}) async-start(f32[64,1,512]{2,1,0:T(1,128)} %broadcast_in_dim.14), calls=%async_computation | async-start | bytes 262144 | tf_op jit(solution)/shard_map/all_to_all | solution.py:39
  29.0 9.1 %collective-permute-start.7 = (bf16[1,32,384]{2,1,0:T(8,128)(2,1)S(1)}, bf16[1,32,384]{2,1,0:T(8,128)(2,1)S(1)}, u32[]{:S(2)}, u32[]{:S(2)}) collective-permute-start(bf16[1,32,384]{2,1,0:T(8,128)(2,1)S(1)} %get-tuple-element.95), channel_id=1, source_target_pairs={{0,1},{1,2},{2,3},{3,4},{4,5},{5,6},{6,7},{7,8},{8,9},{9,10},{10,1... | collective-permute-start | bytes 73736 | tf_op jit(solution)/shard_map/ppermute | solution.py:28
  40.1 3.1 collective-permute-start.1
  42.6 7.0 collective-permute-start
  49.8 4.8 collective-permute-start.2
  54.8 2.0 copy-start.9
  54.8 2.0 copy-start.10
  304.3 1.0 copy-start.33
  304.5 9.9 %copy-start.4 = (bf16[768,384]{1,0:T(8,128)(2,1)}, bf16[768,384]{1,0:T(8,128)(2,1)S(1)}, u32[]{:S(2)}) copy-start(bf16[768,384]{1,0:T(8,128)(2,1)S(1)} %get-tuple-element.126) | copy-start | bytes 1769476
  304.6 10.3 %copy-start = (bf16[768,384]{1,0:T(8,128)(2,1)}, bf16[768,384]{1,0:T(8,128)(2,1)S(1)}, u32[]{:S(2)}) copy-start(bf16[768,384]{1,0:T(8,128)(2,1)S(1)} %get-tuple-element.125) | copy-start | bytes 1769476
  305.9 9.9 %copy-start.2 = (bf16[768,384]{1,0:T(8,128)(2,1)}, bf16[768,384]{1,0:T(8,128)(2,1)S(1)}, u32[]{:S(2)}) copy-start(bf16[768,384]{1,0:T(8,128)(2,1)S(1)} %get-tuple-element.124) | copy-start | bytes 1769476
  306.1 1.0 copy-start.31
  306.3 4.1 copy-start.6
  306.4 1.2 copy-start.30
  307.1 1.0 copy-start.29
  307.6 1.0 copy-start.28
  308.1 1.0 copy-start.27
  308.6 1.0 copy-start.26
  309.6 1.0 copy-start.32
  310.0 4.0 copy-start.38
  310.6 3.8 copy-start.40
  311.0 8.7 %collective-permute-start.3 = (bf16[256,384]{1,0:T(8,128)(2,1)S(1)}, bf16[256,384]{1,0:T(8,128)(2,1)S(1)}, u32[]{:S(2)}, u32[]{:S(2)}) collective-permute-start(bf16[256,384]{1,0:T(8,128)(2,1)S(1)} %fusion.5), channel_id=1, source_target_pairs={{0,128},{64,192},{128,0},{192,64},{1,129},{65,193},{129,1},{193,65... | collective-permute-start | bytes 589832 | tf_op jit(solution)/shard_map/ppermute | solution.py:18
  316.6 1.0 copy-start.34
  318.0 17.6 %copy-start.42 = (bf16[8,32,384]{2,1,0:T(8,128)(2,1)S(1)}, bf16[8,32,384]{2,1,0:T(8,128)(2,1)}, u32[]{:S(2)}) copy-start(bf16[8,32,384]{2,1,0:T(8,128)(2,1)} %get-tuple-element.81) | copy-start | bytes 589828
  319.8 96.0 %copy-start.24 = (bf16[256,384]{1,0:T(8,128)(2,1)}, bf16[256,384]{1,0:T(8,128)(2,1)S(1)}, u32[]{:S(2)}) copy-start(bf16[256,384]{1,0:T(8,128)(2,1)S(1)} %collective-permute-done.3) | copy-start | bytes 589828
  328.2 53.3 %all-to-all-start.1 = ((f32[64,1,512]{2,1,0:T(1,128)}), f32[64,1,512]{2,1,0:T(1,128)}, u32[]{:S(2)}, u32[]{:S(2)}) async-start(f32[64,1,512]{2,1,0:T(1,128)} %broadcast_in_dim.15), calls=%async_computation.1 | async-start | bytes 262144 | tf_op jit(solution)/shard_map/all_to_all | solution.py:39
  335.5 281.0 %reduce-scatter.4.cloned.1.call-start = ((), (), s32[]{:S(2)}) async-start(), calls=%async_computation.6 | async-start | bytes 11943936 | tf_op jit(solution)/shard_map/reduce_scatter | solution.py:61
  338.0 50.8 %collective-permute-start.9 = (bf16[256,384]{1,0:T(8,128)(2,1)}, bf16[256,384]{1,0:T(8,128)(2,1)}, u32[]{:S(2)}, u32[]{:S(2)}) collective-permute-start(bf16[256,384]{1,0:T(8,128)(2,1)} %get-tuple-element.74), channel_id=1, source_target_pairs={{0,64},{64,0},{128,192},{192,128},{1,65},{65,1},{129,193},{193,129... | collective-permute-start | bytes 589832 | tf_op jit(solution)/shard_map/ppermute | solution.py:18
  388.7 27.0 %copy-start.49 = (f32[384]{0:T(512)S(1)}, f32[384]{0:T(512)}, u32[]{:S(2)}) copy-start(f32[384]{0:T(512)} %mul.444) | copy-start | bytes 4612
  388.7 27.0 %copy-start.50 = (f32[384]{0:T(512)S(1)}, f32[384]{0:T(512)}, u32[]{:S(2)}) copy-start(f32[384]{0:T(512)} %sub.99) | copy-start | bytes 4612
  417.0 8.8 %copy-start.23 = (bf16[256,384]{1,0:T(8,128)(2,1)}, bf16[256,384]{1,0:T(8,128)(2,1)S(1)}, u32[]{:S(2)}) copy-start(bf16[256,384]{1,0:T(8,128)(2,1)S(1)} %get-tuple-element.88) | copy-start | bytes 589828
  417.0 3.6 collective-permute-start.5
  418.8 7.0 collective-permute-start.4
  418.8 12.0 %collective-permute-start.10 = (bf16[256,384]{1,0:T(8,128)(2,1)S(1)}, bf16[256,384]{1,0:T(8,128)(2,1)}, u32[]{:S(2)}, u32[]{:S(2)}) collective-permute-start(bf16[256,384]{1,0:T(8,128)(2,1)S(1)} %get-tuple-element.87), channel_id=1, source_target_pairs={{0,128},{64,192},{128,0},{192,64},{1,129},{65,193},{129,1},{193,65... | collective-permute-start | bytes 589832 | tf_op jit(solution)/shard_map/ppermute | solution.py:18
  420.6 6.0 copy-start.43
  426.7 5.7 collective-permute-start.6
  471.8 1.5 copy-start.15
  473.3 1.0 copy-start.16
  474.4 1.0 copy-start.17
  475.4 1.0 copy-start.18
  476.4 1.0 copy-start.19
  477.5 1.0 copy-start.20
  478.5 1.0 copy-start.21
  479.6 1.0 copy-start.22
  505.8 1.3 copy-start.51
  505.8 164.7 %all-reduce.9.cloned.1.call-start = ((), (), s32[]{:S(2)}) async-start(), calls=%async_computation.7 | async-start | bytes 2654208
  505.9 3.7 collective-permute-start.12
  508.3 7.2 collective-permute-start.11
  515.8 1.1 copy-start.5
  516.6 1.1 copy-start.1
  517.3 1.1 copy-start.3
  519.5 1.1 copy-start.7
  520.0 6.7 copy-start.12
  520.0 6.7 copy-start.14
  521.8 94.7 %collective-permute-start.13 = (bf16[256,384]{1,0:T(8,128)(2,1)}, bf16[256,384]{1,0:T(8,128)(2,1)}, u32[]{:S(2)}, u32[]{:S(2)}) collective-permute-start(bf16[256,384]{1,0:T(8,128)(2,1)} %get-tuple-element.72), channel_id=1, source_target_pairs={{0,64},{64,0},{128,192},{192,128},{1,65},{65,1},{129,193},{193,129... | collective-permute-start | bytes 589832 | tf_op jit(solution)/shard_map/ppermute | solution.py:18
  530.4 86.1 %copy-start.41 = (bf16[256,384]{1,0:T(8,128)(2,1)S(1)}, bf16[256,384]{1,0:T(8,128)(2,1)}, u32[]{:S(2)}) copy-start(bf16[256,384]{1,0:T(8,128)(2,1)} %get-tuple-element.71) | copy-start | bytes 589828
  530.4 86.1 %copy-start.46 = (f32[384]{0:T(512)S(1)}, f32[384]{0:T(512)}, u32[]{:S(2)}) copy-start(f32[384]{0:T(512)} %copy-done.45) | copy-start | bytes 4612
  530.4 86.1 %copy-start.48 = (f32[384]{0:T(512)S(1)}, f32[384]{0:T(512)}, u32[]{:S(2)}) copy-start(f32[384]{0:T(512)} %copy-done.47) | copy-start | bytes 4612
  619.2 53.9 %copy-start.8 = (bf16[768,384]{1,0:T(8,128)(2,1)S(1)}, bf16[768,384]{1,0:T(8,128)(2,1)}, u32[]{:S(2)}) copy-start(bf16[768,384]{1,0:T(8,128)(2,1)} %copy-done.6) | copy-start | bytes 1769476
  619.2 53.9 %copy-start.25 = (bf16[256,384]{1,0:T(8,128)(2,1)S(1)}, bf16[256,384]{1,0:T(8,128)(2,1)}, u32[]{:S(2)}) copy-start(bf16[256,384]{1,0:T(8,128)(2,1)} %copy-done.24) | copy-start | bytes 589828
  619.2 18.4 %all-to-all-start.3 = ((f32[64,1,512]{2,1,0:T(1,128)}), f32[64,1,512]{2,1,0:T(1,128)S(1)}, u32[]{:S(2)}, u32[]{:S(2)}) async-start(f32[64,1,512]{2,1,0:T(1,128)} %broadcast_in_dim.17), calls=%async_computation.3 | async-start | bytes 262144 | tf_op jit(solution)/shard_map/all_to_all | solution.py:39
  627.8 83.2 %all-reduce.11.cloned.1.call-start = ((), (), s32[]{:S(2)}) async-start(), calls=%async_computation.8 | async-start | bytes 663552
  (10 other events, 8.0 us)
Sparse Core Ops, SparseCore 0:
  9.8 274.3 all-gather.1
  505.9 110.5 reduce-scatter.3
  618.9 51.5 all-reduce.8
  672.9 38.0 all-reduce.10
where the time goes:
time: 727 us; the launch traced here: 720 us
  waiting for transfers between devices  418 us (57%)
  local copies, waits for them, and re-layouts  119 us (16%)
  starting transfers between devices  97.2 us (13%)
  other arithmetic  25.8 us (4%)
  matrix products  22.6 us (3%)
  blocking collectives  20.4 us (3%)
  between operations  17 us (2%)
    all_gather x1, waiting for transfers between devices, per_device(): weights = lax.all_gather(conv_weight, FSDP, axis=0, tiled=True)  227 us
    reduce_scatter x1, waiting for transfers between devices, reduced_to_own(): tiles = lax.psum_scatter(tiles, axes[k], scatter_dimension=0, tiled=True)  85.7 us
    unnamed x6, waiting for transfers between devices  68.4 us
    ppermute x6, starting transfers between devices, from_partner(): return lax.ppermute(value, axis, pairs)  60.8 us
    dot_general x18, local copies, waits for them, and re-layouts, per_device(): lax.dot_general(slab, chosen_slope, (((0,), (0,)), ((), ())), preferred_e...  34.2 us
    ppermute x4, waiting for transfers between devices, padded_2(): lax.ppermute(tail, axis, [(i, (i + 1) % count) for i in range(count)])  25.7 us
    all_to_all x3, starting transfers between devices, copy_for_each(): return lax.all_to_all(copies, axis, split_axis=0, concat_axis=0, tiled=True)  20.5 us
    all_to_all x1, blocking collectives, copy_for_each(): return lax.all_to_all(copies, axis, split_axis=0, concat_axis=0, tiled=True)  20.4 us
  transfers between devices with their start and end apart: 21, of which 13 were waited for; matrix products, arithmetic and copies ran while one was open for 6% of the time, Pallas kernels for 0%

commit v1 on v0

--- a/solution.py
+++ b/solution.py
@@ -193,7 +193,14 @@
         through = mask_flat * (scale[None, :, None] * centred).reshape(tok, half)
         return (grads.astype(jnp.float32) + through, slope)
 
-    weights = lax.all_gather(conv_weight, FSDP, axis=0, tiled=True)
+    def settle_the_cubes(a0, lane_axis):
+        nodes = []
+        for _ in range(lax.axis_size(lane_axis)):
+            nodes.append(a0)
+        ready = lax.all_to_all(jnp.stack(nodes, 0), lane_axis, 0, 0)
+        return jnp.concatenate(ready, 0)
+
+    weights = settle_the_cubes(conv_weight, FSDP)
     start = (signals.astype(jnp.float32) * mask_flat).astype(jnp.bfloat16)
     first_out, first_cache = forward(start, weights)
     handed = section_swap(first_out, 1)

time: 727 us -> 585 us (0.80)
  waiting for transfers between devices: 418 us -> 332 us
  starting transfers between devices: 97.2 us -> 58.6 us
  local copies, waits for them, and re-layouts: 119 us -> 88.7 us
  blocking collectives: 20.4 us -> 37.5 us
  other arithmetic: 25.8 us -> 10.9 us
  matrix products: 22.6 us -> 33.1 us
    all_gather x1 -> x0, waiting for transfers between devices: 227 us -> none  [per_device(): weights = lax.all_gather(conv_weight, FSDP, axis=0, tiled=True)]
    ppermute x4, waiting for transfers between devices: 0.58 us -> 142 us  [padded_2(): lax.ppermute(head, axis, [((i + 1) % count, i) for i in range(count)])]
    ppermute x6, starting transfers between devices: 60.8 us -> 20.9 us  [from_partner(): return lax.ppermute(value, axis, pairs)]
    slice x1 -> x0, local copies, waits for them, and re-layouts: 20.1 us -> none  [forward(): weights[:, tap, :]]
    all_to_all x1 -> x2, blocking collectives: 20.4 us -> 37.5 us  [copy_for_each(): return lax.all_to_all(copies, axis, split_axis=0, concat_axis=0, tiled=True)]
    unnamed x112 -> x48, local copies, waits for them, and re-layouts: 18.5 us -> 6.06 us
    reshape x0 -> x1, local copies, waits for them, and re-layouts: none -> 9.53 us  [settle_the_cubes(): return jnp.concatenate(ready, 0)]
    all_to_all x3 -> x2, waiting for transfers between devices: 10 us -> 14.8 us  [copy_for_each(): return lax.all_to_all(copies, axis, split_axis=0, concat_axis=0, tiled=True)]
  transfers between devices with their start and end apart: 21 -> 20, of which waited for: 13 -> 14; matrix products, arithmetic and copies ran while one was open for 6% -> 5% of each run, Pallas kernels for 0% -> 0%
where the time goes in v1:
time: 585 us; the launch traced here: 577 us
  waiting for transfers between devices  332 us (57%)
  local copies, waits for them, and re-layouts  88.7 us (15%)
  starting transfers between devices  58.6 us (10%)
  blocking collectives  37.5 us (6%)
  matrix products  33.1 us (6%)
  between operations  16.9 us (3%)
  other arithmetic  10.9 us (2%)
    ppermute x4, waiting for transfers between devices, padded_2(): lax.ppermute(head, axis, [((i + 1) % count, i) for i in range(count)])  142 us
    reduce_scatter x1, waiting for transfers between devices, reduced_to_own(): tiles = lax.psum_scatter(tiles, axes[k], scatter_dimension=0, tiled=True)  84.6 us
    unnamed x5, waiting for transfers between devices  68.6 us
    all_to_all x2, blocking collectives, copy_for_each(): return lax.all_to_all(copies, axis, split_axis=0, concat_axis=0, tiled=True)  37.5 us
    dot_general x18, local copies, waits for them, and re-layouts, per_device(): lax.dot_general(slab, chosen_slope, (((0,), (0,)), ((), ())), preferred_e...  27.8 us
    ppermute x6, starting transfers between devices, from_partner(): return lax.ppermute(value, axis, pairs)  20.9 us
    ppermute x4, waiting for transfers between devices, padded_2(): lax.ppermute(tail, axis, [(i, (i + 1) % count) for i in range(count)])  19.9 us
    all_to_all x2, starting transfers between devices, copy_for_each(): return lax.all_to_all(copies, axis, split_axis=0, concat_axis=0, tiled=True)  18.9 us
  transfers between devices with their start and end apart: 20, of which 14 were waited for; matrix products, arithmetic and copies ran while one was open for 5% of the time, Pallas kernels for 0%

profile of v1, /device:TPU:1, one launch (start us, length us, event | category | flops | bytes accessed | tf_op | source)
XLA Modules:
  0.0 577.5 jit_solution(7129339214259562767)
XLA Ops:
  10.3 1.1 fusion.11
  12.2 23.2 %all_to_all.29 = f32[64,1,512]{2,1,0:T(1,128)S(1)} all-to-all(f32[64,1,512]{2,1,0:T(1,128)S(1)} %broadcast_in_dim.14), channel_id=1, replica_groups=mesh['section'=4,'fsdp_0'=8,'fsdp_1'=2,'fsdp_2'=4] {'fsdp_0','fsdp_1','f..., dimensions={0} | all-to-all | bytes 262144 | tf_op jit(solution)/shard_map/all_to_all | solution.py:39
  35.4 4.4 stack.4
  39.8 5.7 all-to-all-start.1
  45.6 5.6 collective-permute-start.8
  51.1 141.3 %collective-permute-done.8 = bf16[1,32,384]{2,1,0:T(8,128)(2,1)S(1)} collective-permute-done((bf16[1,32,384]{2,1,0:T(8,128)(2,1)S(1)}, bf16[1,32,384]{2,1,0:T(8,128)(2,1)S(1)}, u32[]{:S(2)}, u32[]{:S(2)}) %collective-permute-start.8) | collective-permute-done | bytes 24608 | tf_op jit(solution)/shard_map/ppermute | solution.py:30
  192.5 2.7 collective-permute-done.7
  196.1 4.1 collective-permute-start.1
  201.2 6.7 %collective-permute-done = bf16[1,32,384]{2,1,0:T(8,128)(2,1)S(1)} collective-permute-done((bf16[1,32,384]{2,1,0:T(8,128)(2,1)S(1)}, bf16[1,32,384]{2,1,0:T(8,128)(2,1)S(1)}, u32[]{:S(2)}, u32[]{:S(2)}) %collective-permute-start) | collective-permute-done | bytes 24608 | tf_op jit(solution)/shard_map/ppermute | solution.py:28
  208.0 4.3 collective-permute-start.2
  213.8 1.5 fusion.74
  215.2 6.8 %copy.62 = bf16[64,12,9,384]{3,1,0,2:T(8,128)(2,1)} copy(bf16[64,12,9,384]{3,1,2,0:T(8,128)(2,1)} %all-to-all-done.1) | data formatting | bytes 10616832 | tf_op jit(solution)/shard_map/all_to_all | solution.py:200
  222.0 9.5 %reshape.494 = bf16[768,9,384]{2,0,1:T(8,128)(2,1)} reshape(bf16[64,12,9,384]{3,1,0,2:T(8,128)(2,1)} %copy.62) | data formatting | bytes 10616832 | tf_op jit(solution)/shard_map/reshape | solution.py:201
  231.5 1.7 fusion.78
  233.2 1.7 convolution_add_fusion.30
  235.0 1.5 convolution_add_fusion.29
  236.5 1.5 convolution_add_fusion.28
  239.9 2.5 collective-permute-start.3
  245.7 1.9 collective-permute-done.3
  249.1 10.5 %all-to-all-start.2 = ((f32[64,1,512]{2,1,0:T(1,128)}), f32[64,1,512]{2,1,0:T(1,128)S(1)}, u32[]{:S(2)}, u32[]{:S(2)}) async-start(f32[64,1,512]{2,1,0:T(1,128)} %broadcast_in_dim.15), calls=%async_computation.2 | async-start | bytes 262144 | tf_op jit(solution)/shard_map/all_to_all | solution.py:39
  259.6 1.5 convolution_add_fusion.7
  261.1 1.6 collective-permute-start.9
  262.7 6.6 %all-to-all-done.2 = f32[64,1,512]{2,1,0:T(1,128)S(1)} async-done(((f32[64,1,512]{2,1,0:T(1,128)}), f32[64,1,512]{2,1,0:T(1,128)S(1)}, u32[]{:S(2)}, u32[]{:S(2)}) %all-to-all-start.2) | async-done | bytes 131104 | tf_op jit(solution)/shard_map/all_to_all | solution.py:39
  271.1 14.3 %all_to_all.30 = f32[64,1,512]{2,1,0:T(1,128)S(1)} all-to-all(f32[64,1,512]{2,1,0:T(1,128)S(1)} %broadcast_in_dim.16), channel_id=1, replica_groups=mesh['section'=4,'fsdp_0'=8,'fsdp_1'=2,'fsdp_2'=4] {'fsdp_0','fsdp_1','f..., dimensions={0} | all-to-all | bytes 262144 | tf_op jit(solution)/shard_map/all_to_all | solution.py:39
  286.4 1.9 collective-permute-start.5
  288.3 2.5 collective-permute-start.10
  290.8 4.5 collective-permute-done.4
  295.4 4.5 collective-permute-start.6
  301.5 1.5 fusion.97
  303.9 1.1 dot_general.226
  305.9 1.1 dot_general.230
  307.9 1.1 dot_general.234
  309.0 1.9 copy.69
  310.9 1.9 dot_general.238
  312.8 1.9 copy.70
  314.7 1.9 dot_general.242
  316.6 1.9 copy.71
  318.5 1.9 dot_general.246
  320.4 1.9 copy.72
  322.3 1.9 dot_general.250
  324.2 1.9 copy.73
  326.1 1.9 dot_general.254
  328.9 1.9 dot_general.258
  332.2 1.5 bitcast_dynamic-update-slice_fusion.5
  333.7 1.5 bitcast_dynamic-update-slice_fusion.4
  336.9 11.2 %copy.75 = f32[8,4,2,12,9,384]{5,2,1,0,4,3:T(2,128)} copy(f32[8,4,2,12,9,384]{5,3,1,2,0,4:T(8,128)S(1)} %bitcast.231) | data formatting | bytes 21233664 | tf_op jit(solution)/shard_map/transpose | solution.py:58
  348.2 13.4 %reshape.546 = f32[64,12,9,384]{3,0,2,1:T(8,128)} reshape(f32[8,4,2,12,9,384]{5,2,1,0,4,3:T(2,128)} %copy.75) | data formatting | bytes 21233664 | tf_op jit(solution)/shard_map/reshape | solution.py:59
  364.1 1.3 collective-permute-start.11
  365.4 5.9 %collective-permute-done.11 = bf16[1,32,384]{2,1,0:T(8,128)(2,1)S(1)} collective-permute-done((bf16[1,32,384]{2,1,0:T(8,128)(2,1)S(1)}, bf16[1,32,384]{2,1,0:T(8,128)(2,1)S(1)}, u32[]{:S(2)}, u32[]{:S(2)}) %collective-permute-start.11) | collective-permute-done | bytes 24608 | tf_op jit(solution)/shard_map/ppermute | solution.py:28
  371.6 1.6 fusion.79
  373.2 1.5 fusion.75
  374.7 1.5 convolution_add_fusion.6
  376.1 1.5 convolution_add_fusion.5
  380.3 5.5 collective-permute-start.13
  389.2 84.6 %reduce-scatter.4.cloned.1.call-done = f32[8,12,9,384]{3,0,2,1:T(8,128)} async-done(((f32[64,12,9,384]{3,0,2,1:T(8,128)}), f32[8,12,9,384]{3,0,2,1:T(8,128)}) %reduce-scatter.4.cloned.1.call-update) | async-done | bytes 1327120 | tf_op jit(solution)/shard_map/reduce_scatter | solution.py:61
  473.8 1.2 fusion.91
  476.4 8.4 %all-to-all-start.4 = ((f32[64,1,512]{2,1,0:T(1,128)}), f32[64,1,512]{2,1,0:T(1,128)S(1)}, u32[]{:S(2)}, u32[]{:S(2)}) async-start(f32[64,1,512]{2,1,0:T(1,128)} %broadcast_in_dim.17), calls=%async_computation.4 | async-start | bytes 262144 | tf_op jit(solution)/shard_map/all_to_all | solution.py:39
  484.9 1.5 convolution_add_fusion.16
  486.4 8.2 %all-to-all-done.4 = f32[64,1,512]{2,1,0:T(1,128)S(1)} async-done(((f32[64,1,512]{2,1,0:T(1,128)}), f32[64,1,512]{2,1,0:T(1,128)S(1)}, u32[]{:S(2)}, u32[]{:S(2)}) %all-to-all-start.4) | async-done | bytes 131104 | tf_op jit(solution)/shard_map/all_to_all | solution.py:39
  495.0 32.6 %all-reduce.9.cloned.1.call-done = f32[8,12,9,384]{3,0,2,1:T(8,128)} async-done(((f32[8,12,9,384]{3,0,2,1:T(8,128)}), f32[8,12,9,384]{3,0,2,1:T(8,128)}) %all-reduce.9.cloned.1.call-update) | async-done | bytes 1327120
  527.6 2.2 constant_dynamic-slice_fusion.1
  530.2 2.3 fusion.7
  532.4 35.9 %all-reduce.11.cloned.1.call-done = f32[2,12,9,384]{3,0,2,1:T(2,128)} async-done(((f32[2,12,9,384]{3,0,2,1:T(2,128)}), f32[2,12,9,384]{3,0,2,1:T(2,128)}) %all-reduce.11.cloned.1.call-update) | async-done | bytes 331792
  568.3 1.7 constant_dynamic-slice_fusion
  (219 shorter events, 34.5 us)
Async XLA Ops:
  39.8 175.4 %all-to-all-start.1 = ((bf16[64,12,9,384]{3,1,2,0:T(8,128)(2,1)}), bf16[64,12,9,384]{3,1,2,0:T(8,128)(2,1)}, u32[]{:S(2)}, u32[]{:S(2)}) async-start(bf16[64,12,9,384]{3,1,2,0:T(8,128)(2,1)} %stack.4), calls=%async_computation.1 | async-start | bytes 14155776 | tf_op jit(solution)/shard_map/all_to_all | solution.py:200
  45.6 146.9 %collective-permute-start.8 = (bf16[1,32,384]{2,1,0:T(8,128)(2,1)S(1)}, bf16[1,32,384]{2,1,0:T(8,128)(2,1)S(1)}, u32[]{:S(2)}, u32[]{:S(2)}) collective-permute-start(bf16[1,32,384]{2,1,0:T(8,128)(2,1)S(1)} %get-tuple-element.87), channel_id=1, source_target_pairs={{1,0},{2,1},{3,2},{4,3},{5,4},{6,5},{7,6},{8,7},{9,8},{10,9},{11,1... | collective-permute-start | bytes 73736 | tf_op jit(solution)/shard_map/ppermute | solution.py:30
  51.1 144.1 %collective-permute-start.7 = (bf16[1,32,384]{2,1,0:T(8,128)(2,1)S(1)}, bf16[1,32,384]{2,1,0:T(8,128)(2,1)S(1)}, u32[]{:S(2)}, u32[]{:S(2)}) collective-permute-start(bf16[1,32,384]{2,1,0:T(8,128)(2,1)S(1)} %get-tuple-element.86), channel_id=1, source_target_pairs={{0,1},{1,2},{2,3},{3,4},{4,5},{5,6},{6,7},{7,8},{8,9},{9,10},{10,1... | collective-permute-start | bytes 73736 | tf_op jit(solution)/shard_map/ppermute | solution.py:28
  196.1 5.0 collective-permute-start.1
  201.0 6.9 %collective-permute-start = (bf16[1,32,384]{2,1,0:T(8,128)(2,1)S(1)}, bf16[1,32,384]{2,1,0:T(8,128)(2,1)S(1)}, u32[]{:S(2)}, u32[]{:S(2)}) collective-permute-start(bf16[1,32,384]{2,1,0:T(8,128)(2,1)S(1)} %get-tuple-element.90), channel_id=1, source_target_pairs={{0,1},{1,2},{2,3},{3,4},{4,5},{5,6},{6,7},{7,8},{8,9},{9,10},{10,1... | collective-permute-start | bytes 73736 | tf_op jit(solution)/shard_map/ppermute | solution.py:28
  208.0 5.5 collective-permute-start.2
  231.5 6.4 %copy-start = (bf16[768,9,384]{2,0,1:T(8,128)(2,1)S(1)}, bf16[768,9,384]{2,0,1:T(8,128)(2,1)}, u32[]{:S(2)}) copy-start(bf16[768,9,384]{2,0,1:T(8,128)(2,1)} %reshape.494) | copy-start | bytes 15925252
  235.0 4.5 copy-start.7
  236.5 6.0 %copy-start.12 = (bf16[8,32,384]{2,1,0:T(8,128)(2,1)S(1)}, bf16[8,32,384]{2,1,0:T(8,128)(2,1)}, u32[]{:S(2)}) copy-start(bf16[8,32,384]{2,1,0:T(8,128)(2,1)} %get-tuple-element.77) | copy-start | bytes 589828
  237.9 4.9 copy-start.14
  238.3 4.9 copy-start.11
  239.1 4.5 copy-start.10
  239.9 7.7 %collective-permute-start.3 = (bf16[256,384]{1,0:T(8,128)(2,1)S(1)}, bf16[256,384]{1,0:T(8,128)(2,1)S(1)}, u32[]{:S(2)}, u32[]{:S(2)}) collective-permute-start(bf16[256,384]{1,0:T(8,128)(2,1)S(1)} %fusion.5), channel_id=1, source_target_pairs={{0,128},{64,192},{128,0},{192,64},{1,129},{65,193},{129,1},{193,65... | collective-permute-start | bytes 589832 | tf_op jit(solution)/shard_map/ppermute | solution.py:18
  242.4 2.0 copy-start.9
  243.2 1.7 copy-start.8
  243.6 1.7 copy-start.13
  244.0 15.6 %copy-start.16 = (bf16[8,32,384]{2,1,0:T(8,128)(2,1)S(1)}, bf16[8,32,384]{2,1,0:T(8,128)(2,1)}, u32[]{:S(2)}) copy-start(bf16[8,32,384]{2,1,0:T(8,128)(2,1)} %get-tuple-element.72) | copy-start | bytes 589828
  244.9 41.3 %copy-start.15 = (bf16[256,384]{1,0:T(8,128)(2,1)S(1)}, bf16[256,384]{1,0:T(8,128)(2,1)}, u32[]{:S(2)}) copy-start(bf16[256,384]{1,0:T(8,128)(2,1)} %param.3) | copy-start | bytes 589828
  247.6 52.4 %copy-start.5 = (bf16[256,384]{1,0:T(8,128)(2,1)}, bf16[256,384]{1,0:T(8,128)(2,1)S(1)}, u32[]{:S(2)}) copy-start(bf16[256,384]{1,0:T(8,128)(2,1)S(1)} %collective-permute-done.3) | copy-start | bytes 589828
  249.1 20.2 %all-to-all-start.2 = ((f32[64,1,512]{2,1,0:T(1,128)}), f32[64,1,512]{2,1,0:T(1,128)S(1)}, u32[]{:S(2)}, u32[]{:S(2)}) async-start(f32[64,1,512]{2,1,0:T(1,128)} %broadcast_in_dim.15), calls=%async_computation.2 | async-start | bytes 262144 | tf_op jit(solution)/shard_map/all_to_all | solution.py:39
  259.6 214.2 %reduce-scatter.4.cloned.1.call-start = ((), (), s32[]{:S(2)}) async-start(), calls=%async_computation.6 | async-start | bytes 11943936 | tf_op jit(solution)/shard_map/reduce_scatter | solution.py:61
  261.1 8.9 %collective-permute-start.9 = (bf16[256,384]{1,0:T(8,128)(2,1)S(1)}, bf16[256,384]{1,0:T(8,128)(2,1)S(1)}, u32[]{:S(2)}, u32[]{:S(2)}) collective-permute-start(bf16[256,384]{1,0:T(8,128)(2,1)S(1)} %get-tuple-element.65), channel_id=1, source_target_pairs={{0,64},{64,0},{128,192},{192,128},{1,65},{65,1},{129,193},{193,129... | collective-permute-start | bytes 589832 | tf_op jit(solution)/shard_map/ppermute | solution.py:18
  286.4 4.4 collective-permute-start.5
  288.3 7.0 %collective-permute-start.4 = (bf16[1,32,384]{2,1,0:T(8,128)(2,1)S(1)}, bf16[1,32,384]{2,1,0:T(8,128)(2,1)S(1)}, u32[]{:S(2)}, u32[]{:S(2)}) collective-permute-start(bf16[1,32,384]{2,1,0:T(8,128)(2,1)S(1)} %get-tuple-element.88), channel_id=1, source_target_pairs={{0,1},{1,2},{2,3},{3,4},{4,5},{5,6},{6,7},{7,8},{8,9},{9,10},{10,1... | collective-permute-start | bytes 73736 | tf_op jit(solution)/shard_map/ppermute | solution.py:28
  288.3 11.6 %collective-permute-start.10 = (bf16[256,384]{1,0:T(8,128)(2,1)S(1)}, bf16[256,384]{1,0:T(8,128)(2,1)S(1)}, u32[]{:S(2)}, u32[]{:S(2)}) collective-permute-start(bf16[256,384]{1,0:T(8,128)(2,1)S(1)} %get-tuple-element.78), channel_id=1, source_target_pairs={{0,128},{64,192},{128,0},{192,64},{1,129},{65,193},{129,1},{193,65... | collective-permute-start | bytes 589832 | tf_op jit(solution)/shard_map/ppermute | solution.py:18
  295.4 5.7 collective-permute-start.6
  299.9 0.7 copy-start.17
  330.8 4.3 copy-start.1
  331.3 4.3 copy-start.2
  331.7 4.3 copy-start.3
  332.1 4.3 copy-start.4
  361.6 0.7 copy-start.19
  361.6 1.3 copy-start.18
  361.6 16.0 %slice-start = ((s8[5308416]{0:T(1024)(128)(4,1)}), s8[1114112]{0:T(1024)(128)(4,1)S(1)}, s32[]{:S(2)}) async-start(s8[5308416]{0:T(1024)(128)(4,1)} %bitcast.229), calls=%async_computation.9 | async-start | bytes 2228224
  361.6 166.0 %all-reduce.9.cloned.1.call-start = ((), (), s32[]{:S(2)}) async-start(), calls=%async_computation.7 | async-start | bytes 2654208
  361.7 3.7 collective-permute-start.12
  364.1 7.2 %collective-permute-start.11 = (bf16[1,32,384]{2,1,0:T(8,128)(2,1)S(1)}, bf16[1,32,384]{2,1,0:T(8,128)(2,1)S(1)}, u32[]{:S(2)}, u32[]{:S(2)}) collective-permute-start(bf16[1,32,384]{2,1,0:T(8,128)(2,1)S(1)} %get-tuple-element.82), channel_id=1, source_target_pairs={{0,1},{1,2},{2,3},{3,4},{4,5},{5,6},{6,7},{7,8},{8,9},{9,10},{10,1... | collective-permute-start | bytes 73736 | tf_op jit(solution)/shard_map/ppermute | solution.py:28
  371.3 6.3 %slice-start.1 = ((s8[5308416]{0:T(1024)(128)(4,1)}), s8[4194304]{0:T(1024)(128)(4,1)S(1)}, s32[]{:S(2)}) async-start(s8[5308416]{0:T(1024)(128)(4,1)} %bitcast.229), calls=%async_computation.10 | async-start | bytes 8388608
  380.3 93.5 %collective-permute-start.13 = (bf16[256,384]{1,0:T(8,128)(2,1)}, bf16[256,384]{1,0:T(8,128)(2,1)}, u32[]{:S(2)}, u32[]{:S(2)}) collective-permute-start(bf16[256,384]{1,0:T(8,128)(2,1)} %get-tuple-element.63), channel_id=1, source_target_pairs={{0,64},{64,0},{128,192},{192,128},{1,65},{65,1},{129,193},{193,129... | collective-permute-start | bytes 589832 | tf_op jit(solution)/shard_map/ppermute | solution.py:18
  388.0 142.2 %copy-start.6 = (bf16[256,384]{1,0:T(8,128)(2,1)S(1)}, bf16[256,384]{1,0:T(8,128)(2,1)}, u32[]{:S(2)}) copy-start(bf16[256,384]{1,0:T(8,128)(2,1)} %copy-done.5) | copy-start | bytes 589828
  476.4 18.2 %all-to-all-start.4 = ((f32[64,1,512]{2,1,0:T(1,128)}), f32[64,1,512]{2,1,0:T(1,128)S(1)}, u32[]{:S(2)}, u32[]{:S(2)}) async-start(f32[64,1,512]{2,1,0:T(1,128)} %broadcast_in_dim.17), calls=%async_computation.4 | async-start | bytes 262144 | tf_op jit(solution)/shard_map/all_to_all | solution.py:39
  484.8 83.5 %all-reduce.11.cloned.1.call-start = ((), (), s32[]{:S(2)}) async-start(), calls=%async_computation.8 | async-start | bytes 663552
Sparse Core Ops, SparseCore 0:
  361.8 111.9 reduce-scatter.3
  476.1 51.4 all-reduce.8
  530.2 38.0 all-reduce.10
